TPU v7x, 512 devices: a whole 4x8x8 slice. The times are simulated.
512 devices in a mesh: box: 128 (over z, y, core), coarse: 4 (over x).
Axes of the slice: x: 4, y: 8, z: 8, core: 2. Of those that a mesh axis runs over, the one named last changes fastest.
Arguments:
- points: float32 [128, 8, 3, 256], P('box', 'coarse'), may hold values from 0 to 1
- self_gain: float32 [128, 8, 256], P('box', 'coarse'), may hold values from 1.5 to 4
- pivots: int32 [128, 8, 256], P('box', 'coarse'), may hold values from 0 to 255, each once within a row
- interp: float32 [128, 8, 128, 128], P('box', 'coarse'), may hold values from -0.5 to 0.5
- neighbors: int32 [128, 8, 6], P('box', 'coarse'), may hold values from 0 to 15, as said below
- rhs: float32 [128, 8, 256, 512], P('box', 'coarse'), may hold values from -6 to 6
Outputs:
- solution: float32 [128, 8, 256, 512], P('box', 'coarse')
Inputs may be any that keep to these rules, and one draw needn't show every extreme that they name: `pivots`: each box's row orders all 256 of its points once; the first 128 form its skeleton. `neighbors`: each box lists 6 different boxes; n < 8 names child n of the previous parent, 8 + n child n of the next parent.
All inputs are finite; a program needn't handle non-finite values.
Results may differ from a plain program's by a relative error of at most 0.0003.
Values sent between devices are 32-bit elements; how exact they have to be, the bound alone decides.
No kernel may reach another device: no remote copies, remote signals or barrier semaphores. Data moves between devices by JAX's collectives and lax.ppermute only.
A program may use at most 64 MiB of HBM per device.

v0:
```python
import jax
import jax.numpy as jnp
from jax import lax
from jax.sharding import PartitionSpec as P

NP = 256
CHILD = 8
softening = 0.0025


def shifted_2(block, axis, distance):
    devices = range(lax.axis_size(axis))
    route = [(i - distance, i) for i in devices if i - distance in devices]
    return lax.ppermute(block, axis, route)


def kernel_block(targets, sources):
    difference = targets[:, :, None] - sources[:, None, :]
    return lax.rsqrt(jnp.sum(difference * difference, axis=0) + softening)


def product(left, right):
    return jnp.dot(left, right, precision=lax.Precision.HIGHEST)


def chol_apply(factor, right):
    return jax.scipy.linalg.cho_solve((factor, True), right)


def box_corners(group_ids, child_ids):
    along_x = 2 * group_ids + child_ids % 2
    along_y = child_ids // 2 % 2
    along_z = child_ids // 4
    return jnp.stack([along_x, along_y, along_z], axis=-1).astype(jnp.float32)


def factor_box(located, gains, order, interp, right_side):
    ordered = jnp.take(located, order, axis=1)
    ordered_gain = jnp.take(gains, order, axis=0)
    ordered_rhs = jnp.take(right_side, order, axis=0)
    kernel = kernel_block(ordered, ordered)
    count = ordered.shape[1]
    rank = interp.shape[0]
    matrix = (kernel + jnp.diag(ordered_gain * jnp.sum(kernel, axis=1))) / count
    skel_skel = matrix[:rank, :rank]
    skel_red = matrix[:rank, rank:]
    red_skel = matrix[rank:, :rank]
    red_red = matrix[rank:, rank:]
    shifted = product(interp.T, skel_skel)
    red_block = (
        red_red - product(interp.T, skel_red) - product(red_skel, interp) + product(shifted, interp)
    )
    cross = red_skel - shifted
    red_factor = jnp.linalg.cholesky(red_block)
    coupling = chol_apply(red_factor, cross)
    schur = skel_skel - product(cross.T, coupling)
    reduced = ordered_rhs[rank:] - product(interp.T, ordered_rhs[:rank])
    interior = chol_apply(red_factor, reduced)
    skeleton_rhs = ordered_rhs[:rank] - product(coupling.T, reduced)
    schur_factor = jnp.linalg.cholesky(schur)
    local_solve = chol_apply(schur_factor, skeleton_rhs)
    return (schur_factor, coupling, interior, local_solve, ordered[:, :rank])


def coarse_weights(neighbor_rows, own_child):
    listed = jnp.any(
        neighbor_rows[:, :, None] == jnp.arange(2 * CHILD, dtype=jnp.int32)[None, None, :], axis=1
    ).astype(jnp.float32)
    siblings = (own_child[:, None] != jnp.arange(CHILD, dtype=jnp.int32)[None, :]).astype(
        jnp.float32
    )
    return jnp.concatenate([listed[:, :CHILD], siblings, listed[:, CHILD:]], axis=1)


def coarse_terms(skeleton, cand_pts, cand_rhs, weights):
    blocks = jax.vmap(
        lambda target: jax.vmap(lambda source: kernel_block(target, source))(cand_pts)
    )(skeleton)
    return (
        jnp.einsum(
            "bckl,cln->bkn",
            blocks * weights[:, :, None, None],
            cand_rhs,
            precision=lax.Precision.HIGHEST,
        )
        / NP
    )


def finish_box(schur_factor, coupling, interior, local_solve, correction, interp, order):
    coarse = local_solve - chol_apply(schur_factor, correction)
    redundant = interior - product(coupling, coarse)
    skeletal = coarse - product(interp, redundant)
    ordered = jnp.concatenate([skeletal, redundant], axis=0)
    return jnp.zeros_like(ordered).at[order].set(ordered)


def per_device(points, self_gain, pivots, interp, neighbors, rhs):
    groups_here = points.shape[0]
    children_here = points.shape[1]
    group_ids = lax.axis_index("box") * groups_here + jnp.arange(groups_here, dtype=jnp.int32)
    child_ids = lax.axis_index("coarse") * children_here + jnp.arange(
        children_here, dtype=jnp.int32
    )
    zero_grid = jnp.zeros((groups_here, children_here), jnp.int32)
    located = points + box_corners(group_ids[:, None] + zero_grid, child_ids[None, :])[..., None]
    schur_factor, coupling, interior, local_solve, skeleton = jax.vmap(jax.vmap(factor_box))(
        located, self_gain, pivots, interp, rhs
    )
    full_rhs, full_pts = (
        lax.all_gather(local_solve, "coarse", axis=1, tiled=True),
        lax.all_gather(skeleton, "coarse", axis=1, tiled=True),
    )
    left_rhs, left_pts = shifted_2((full_rhs, full_pts), "box", 1)
    right_rhs, right_pts = shifted_2((full_rhs, full_pts), "box", -1)
    wide_rhs = jnp.concatenate([left_rhs, full_rhs, right_rhs], axis=0)
    wide_pts = jnp.concatenate([left_pts, full_pts, right_pts], axis=0)
    cand_rhs = jnp.concatenate([wide_rhs[:-2], wide_rhs[1:-1], wide_rhs[2:]], axis=1)
    cand_pts = jnp.concatenate([wide_pts[:-2], wide_pts[1:-1], wide_pts[2:]], axis=1)
    weights = jax.vmap(coarse_weights, in_axes=(0, None))(neighbors, child_ids)
    correction = jax.vmap(coarse_terms)(skeleton, cand_pts, cand_rhs, weights)
    return jax.vmap(jax.vmap(finish_box))(
        schur_factor, coupling, interior, local_solve, correction, interp, pivots
    )


def solution(mesh):
    in_specs = (
        P("box", "coarse", None, None),
        P("box", "coarse", None),
        P("box", "coarse", None),
        P("box", "coarse", None, None),
        P("box", "coarse", None),
        P("box", "coarse", None, None),
    )
    out_specs = P("box", "coarse", None, None)
    return jax.shard_map(
        per_device, mesh=mesh, in_specs=in_specs, out_specs=out_specs, check_vma=False
    )
```

profile of v0, /device:TPU:25, one launch (start us, length us, event | category | flops | bytes accessed | tf_op | source)
XLA Modules:
  0.0 234.6 jit_solution(4038636412961429317)
XLA Ops:
  6.6 0.8 fusion.71
  7.3 0.7 fusion.74
  8.3 0.8 broadcast_add_fusion
  9.0 0.1 copy.111
  9.3 3.6 %gather_fusion = f32[512,3]{1,0:T(8,128)S(1)} fusion(f32[1,2,3,256]{2,3,1,0:T(8,128)S(1)} %copy.111, s32[512]{0:T(512)S(1)} %bitcast.209), kind=kCustom, calls=%fused_computation | custom fusion | bytes 18432 | tf_op jit(solution)/shard_map/vmap(vmap(jit(_take)))/gather | solution.py:38
  13.1 0.3 multiply_reduce_fusion.1
  13.4 0.2 copy.115
  13.7 4.7 %gather_fusion.1 = f32[512]{0:T(512)S(1)} fusion(f32[1,2,256]{2,1,0:T(2,128)S(1)} %copy-done.1, s32[512]{0:T(512)S(1)} %bitcast.210), kind=kCustom, calls=%fused_computation.1 | custom fusion | bytes 10240 | tf_op jit(solution)/shard_map/vmap(vmap(jit(_take)))/gather | solution.py:39
  18.4 0.1 fusion.30
  18.5 0.3 fusion.25
  18.8 0.3 fusion.56
  19.1 0.4 fusion.24
  19.5 0.4 fusion.23
  20.0 23.5 %custom-call.27 = f32[1,2,128,128]{3,2,1,0:T(8,128)S(1)} custom-call(f32[1,2,128,128]{3,2,1,0:T(8,128)S(1)} %fusion.49), custom_call_target="Cholesky" | custom-call | tf_op jit(solution)/shard_map/vmap(vmap(jit(cholesky)))/cholesky | solution.py:54
  43.5 0.1 compare_reduce_fusion.1
  43.7 19.7 %custom-call.15 = f32[1,2,1,128,128]{3,4,2,1,0:T(8,128)S(1)} custom-call(f32[1,2,1,128,128]{4,3,2,1,0:T(8,128)S(1)} %fusion.59), custom_call_target="InvertDiagBlocksLowerTriangular" | custom-call | tf_op jit(solution)/shard_map/vmap(vmap(jit(_cho_solve)))/triangular_solve | solution.py:27
  63.4 0.4 fusion.47
  63.8 0.3 fusion.45
  64.1 0.4 fusion.26
  64.6 23.6 %custom-call.28 = f32[1,2,128,128]{3,2,1,0:T(8,128)S(1)} custom-call(f32[1,2,128,128]{3,2,1,0:T(8,128)S(1)} %fusion.41), custom_call_target="Cholesky" | custom-call | tf_op jit(solution)/shard_map/vmap(vmap(jit(cholesky)))/cholesky | solution.py:60
  88.3 0.1 compare_reduce_fusion
  88.5 19.7 %custom-call.29 = f32[1,2,1,128,128]{3,4,2,1,0:T(8,128)S(1)} custom-call(f32[1,2,1,128,128]{4,3,2,1,0:T(8,128)S(1)} %select_bitcast_fusion), custom_call_target="InvertDiagBlocksLowerTriangular" | custom-call | tf_op jit(solution)/shard_map/vmap(vmap(jit(_cho_solve)))/triangular_solve | solution.py:27
  108.2 3.9 %gather_fusion.2 = f32[512,512]{1,0:T(8,128)S(1)} fusion(f32[1,2,256,512]{3,2,1,0:T(8,128)S(1)} %copy-done, s32[512]{0:T(512)S(1)} %bitcast.211), kind=kCustom, calls=%fused_computation.2 | custom fusion | bytes 2103296 | tf_op jit(solution)/shard_map/vmap(vmap(jit(_take)))/gather | solution.py:40
  112.1 0.3 copy.127
  112.6 0.6 fusion.17
  113.2 0.2 copy-done.6
  113.4 0.6 fusion.19
  114.0 0.6 fusion.39
  114.6 1.4 fusion.37
  116.0 40.4 %all-gather.2.cloned.1.call-done = f32[1,8,128,512]{3,2,0,1:T(8,128)} async-done(((f32[1,2,128,512]{3,2,0,1:T(8,128)}), f32[1,8,128,512]{3,2,0,1:T(8,128)}) %all-gather.2.cloned.1.call-update) | async-done | bytes 2097168 | tf_op jit(solution)/shard_map/all_gather | solution.py:111
  156.5 5.2 %collective-permute-start.2 = (f32[1,8,128,512]{3,2,1,0:T(8,128)}, f32[1,8,128,512]{3,2,1,0:T(8,128)S(1)}, u32[]{:S(2)}, u32[]{:S(2)}) collective-permute-start(f32[1,8,128,512]{3,2,1,0:T(8,128)} %bitcast.219), channel_id=1, source_target_pairs={{0,4},{4,8},{8,12},{12,16},{16,20},{20,24},{24,28},{28,32},{32,36}... | collective-permute-start | bytes 6291464 | tf_op jit(solution)/shard_map/ppermute | solution.py:14
  161.7 1.9 collective-permute-start.3
  163.6 9.0 %all_gather.6 = f32[1,8,3,128]{3,0,2,1:T(1,128)S(1)} all-gather(f32[1,2,3,128]{3,0,2,1:T(1,128)S(1)} %copy.134), channel_id=1, replica_groups=mesh['box'=128,'coarse'=4] {'coarse'}, dimensions={1}, use_global_device_ids=true | all-gather | bytes 15360 | tf_op jit(solution)/shard_map/all_gather | solution.py:112
  172.7 7.7 %collective-permute-start = (f32[1,8,3,128]{3,0,2,1:T(1,128)S(1)}, f32[1,8,3,128]{3,0,2,1:T(1,128)S(1)}, u32[]{:S(2)}, u32[]{:S(2)}) collective-permute-start(f32[1,8,3,128]{3,0,2,1:T(1,128)S(1)} %all_gather.6), channel_id=1, source_target_pairs={{0,4},{4,8},{8,12},{12,16},{16,20},{20,24},{24,28},{28,32},{32,36}... | collective-permute-start | bytes 36872 | tf_op jit(solution)/shard_map/ppermute | solution.py:14
  180.4 2.1 collective-permute-start.1
  182.8 0.6 fusion.43
  183.6 1.4 collective-permute-done
  185.0 5.6 %collective-permute-done.1 = f32[1,8,3,128]{3,0,2,1:T(1,128)S(1)} collective-permute-done((f32[1,8,3,128]{3,0,2,1:T(1,128)S(1)}, f32[1,8,3,128]{3,0,2,1:T(1,128)S(1)}, u32[]{:S(2)}, u32[]{:S(2)}) %collective-permute-start.1) | collective-permute-done | bytes 12320 | tf_op jit(solution)/shard_map/ppermute | solution.py:14
  190.6 1.2 multiply_reduce_fusion
  191.8 5.7 %fusion.13 = f32[2,128,512]{2,1,0:T(8,128)S(1)} fusion(f32[1,8,128,512]{3,2,1,0:T(8,128)S(1)} %collective-permute-done.3, f32[1,8,128,512]{3,2,1,0:T(8,128)S(1)} %bitcast.221, f32[1,8,128,512]{3,2,1,0:T(8,128)S(1)} %collective-permute-done.2, f32[2,24,128,128]{3,2,1,0:T(8,128)S(1)} %multiply_reduce_fusion, f32[2,24]{1,0:T(2,128)S(1)} %maximum_bitcast_fusion.7), kind=kOutput, calls=%fused_computation.24 | convolution fusion | flops 4836687872 | bytes 9961664 | tf_op jit(solution)/shard_map/vmap(bckl,cln->bkn)/dot_general | solution.py:80
  197.5 0.6 fusion.35
  198.1 0.6 fusion.20
  198.7 0.6 convolution_bitcast_fusion.1
  199.3 0.6 fusion.21
  199.9 0.6 fusion.22
  200.6 0.1 broadcast.679
  200.7 26.0 %scatter_fusion = f32[2,256,512]{2,1,0:T(8,128)S(1)} fusion(f32[2,256,512]{2,1,0:T(8,128)S(1)} %broadcast.679, s32[512]{0:T(512)S(1)} %bitcast.212, f32[512,512]{1,0:T(8,128)S(1)} %bitcast.214), kind=kCustom, calls=%fused_computation.3 | custom fusion | bytes 3149824 | tf_op jit(solution)/shard_map/vmap(vmap())/scatter | solution.py:95
  226.8 1.0 copy-done.2
  (67 shorter events, 1.7 us)
Async XLA Ops:
  6.5 101.7 %copy-start = (f32[1,2,256,512]{3,2,1,0:T(8,128)S(1)}, f32[1,2,256,512]{3,2,1,0:T(8,128)}, u32[]{:S(2)}) copy-start(f32[1,2,256,512]{3,2,1,0:T(8,128)} %param.14) | copy-start | bytes 3145732
  6.5 11.8 %copy-start.7 = (s32[1,2,256]{2,1,0:T(2,128)S(1)}, s32[1,2,256]{2,1,0:T(2,128)}, u32[]{:S(2)}) copy-start(s32[1,2,256]{2,1,0:T(2,128)} %param.11) | copy-start | bytes 6148
  6.5 7.1 %copy-start.1 = (f32[1,2,256]{2,1,0:T(2,128)S(1)}, f32[1,2,256]{2,1,0:T(2,128)}, u32[]{:S(2)}) copy-start(f32[1,2,256]{2,1,0:T(2,128)} %param.10) | copy-start | bytes 6148
  6.5 150.0 %all-gather.2.cloned.1.call-start = ((), (), s32[]{:S(2)}) async-start(), calls=%async_computation | async-start | bytes 2621440 | tf_op jit(solution)/shard_map/all_gather | solution.py:111
  9.2 9.3 %copy-start.4 = (f32[1,2,128,128]{3,2,1,0:T(8,128)S(1)}, f32[1,2,128,128]{3,2,1,0:T(8,128)}, u32[]{:S(2)}) copy-start(f32[1,2,128,128]{3,2,1,0:T(8,128)} %param.12) | copy-start | bytes 393220
  64.1 24.4 %copy-start.5 = (f32[2,128,128]{2,1,0:T(8,128)}, f32[2,128,128]{2,1,0:T(8,128)S(1)}, u32[]{:S(2)}) copy-start(f32[2,128,128]{2,1,0:T(8,128)S(1)} %fusion.45) | copy-start | bytes 393220
  112.5 0.9 copy-start.6
  112.6 70.0 %copy-start.9 = (s32[1,2,6]{2,1,0:T(2,128)S(1)}, s32[1,2,6]{2,1,0:T(2,128)}, u32[]{:S(2)}) copy-start(s32[1,2,6]{2,1,0:T(2,128)} %param.13) | copy-start | bytes 148
  156.5 35.3 %copy-start.8 = (f32[1,8,128,512]{3,2,0,1:T(8,128)S(1)}, f32[1,8,128,512]{3,2,0,1:T(8,128)}, u32[]{:S(2)}) copy-start(f32[1,8,128,512]{3,2,0,1:T(8,128)} %all-gather.2.cloned.1.call-done) | copy-start | bytes 6291460
  156.5 35.3 %collective-permute-start.2 = (f32[1,8,128,512]{3,2,1,0:T(8,128)}, f32[1,8,128,512]{3,2,1,0:T(8,128)S(1)}, u32[]{:S(2)}, u32[]{:S(2)}) collective-permute-start(f32[1,8,128,512]{3,2,1,0:T(8,128)} %bitcast.219), channel_id=1, source_target_pairs={{0,4},{4,8},{8,12},{12,16},{16,20},{20,24},{24,28},{28,32},{32,36}... | collective-permute-start | bytes 6291464 | tf_op jit(solution)/shard_map/ppermute | solution.py:14
  161.7 30.1 %collective-permute-start.3 = (f32[1,8,128,512]{3,2,1,0:T(8,128)}, f32[1,8,128,512]{3,2,1,0:T(8,128)S(1)}, u32[]{:S(2)}, u32[]{:S(2)}) collective-permute-start(f32[1,8,128,512]{3,2,1,0:T(8,128)} %bitcast.220), channel_id=1, source_target_pairs={{4,0},{8,4},{12,8},{16,12},{20,16},{24,20},{28,24},{32,28},{36,32}... | collective-permute-start | bytes 6291464 | tf_op jit(solution)/shard_map/ppermute | solution.py:14
  172.7 12.3 %collective-permute-start = (f32[1,8,3,128]{3,0,2,1:T(1,128)S(1)}, f32[1,8,3,128]{3,0,2,1:T(1,128)S(1)}, u32[]{:S(2)}, u32[]{:S(2)}) collective-permute-start(f32[1,8,3,128]{3,0,2,1:T(1,128)S(1)} %all_gather.6), channel_id=1, source_target_pairs={{0,4},{4,8},{8,12},{12,16},{16,20},{20,24},{24,28},{28,32},{32,36}... | collective-permute-start | bytes 36872 | tf_op jit(solution)/shard_map/ppermute | solution.py:14
  180.4 10.2 %collective-permute-start.1 = (f32[1,8,3,128]{3,0,2,1:T(1,128)S(1)}, f32[1,8,3,128]{3,0,2,1:T(1,128)S(1)}, u32[]{:S(2)}, u32[]{:S(2)}) collective-permute-start(f32[1,8,3,128]{3,0,2,1:T(1,128)S(1)} %all_gather.6), channel_id=1, source_target_pairs={{4,0},{8,4},{12,8},{16,12},{20,16},{24,20},{28,24},{32,28},{36,32}... | collective-permute-start | bytes 36872 | tf_op jit(solution)/shard_map/ppermute | solution.py:14
  191.8 6.4 %copy-start.3 = (f32[2,128,512]{2,1,0:T(8,128)S(1)}, f32[2,128,512]{2,1,0:T(8,128)}, u32[]{:S(2)}) copy-start(f32[2,128,512]{2,1,0:T(8,128)} %fusion.37) | copy-start | bytes 1572868
  226.8 1.0 copy-start.2
Sparse Core Ops, SparseCore 0:
  116.2 40.2 all-gather.1
where the time goes:
time: 235 us
  other arithmetic  91.5 us (39%)
  waiting for transfers between devices  47.5 us (20%)
  local copies, waits for them, and re-layouts  40.7 us (17%)
  starting transfers between devices  17 us (7%)
  matrix products  14.8 us (6%)
  between operations  14 us (6%)
  blocking collectives  9.05 us (4%)
    all_gather x1, waiting for transfers between devices, per_device(): lax.all_gather(local_solve, 'coarse', axis=1, tiled=True)  40.4 us
    another operation x5, other arithmetic, chol_apply(): return jax.scipy.linalg.cho_solve((factor, True), right)  39.6 us
    scatter x2, local copies, waits for them, and re-layouts, finish_box(): return jnp.zeros_like(ordered).at[order].set(ordered)  26 us
    another operation x4, other arithmetic, factor_box(): schur_factor = jnp.linalg.cholesky(schur)  23.8 us
    another operation x3, other arithmetic, factor_box(): red_factor = jnp.linalg.cholesky(red_block)  23.6 us
    ppermute x4, starting transfers between devices, shifted_2(): return lax.ppermute(block, axis, route)  17 us
    all_gather x1, blocking collectives, per_device(): lax.all_gather(skeleton, 'coarse', axis=1, tiled=True)  9.05 us
    ppermute x4, waiting for transfers between devices, shifted_2(): return lax.ppermute(block, axis, route)  7.02 us
  transfers between devices with their start and end apart: 5, of which 3 were waited for; matrix products, arithmetic and copies ran while one was open for 1% of the time, Pallas kernels for 0%

commit v1 on v0

--- a/solution.py
+++ b/solution.py
@@ -108,7 +108,10 @@
         located, self_gain, pivots, interp, rhs
     )
     full_rhs, full_pts = (
-        lax.all_gather(local_solve, "coarse", axis=1, tiled=True),
+        jnp.concatenate(
+            lax.all_to_all(jnp.stack([local_solve] * lax.axis_size("coarse")), "coarse", 0, 0),
+            axis=1,
+        ),
         lax.all_gather(skeleton, "coarse", axis=1, tiled=True),
     )
     left_rhs, left_pts = shifted_2((full_rhs, full_pts), "box", 1)

time: 235 us -> 216 us (0.919)
  the two profiles are of different devices: /device:TPU:25 before, /device:TPU:249 now
where the time goes in v1:
time: 216 us
  other arithmetic  91.5 us (42%)
  local copies, waits for them, and re-layouts  42.3 us (20%)
  waiting for transfers between devices  32.8 us (15%)
  starting transfers between devices  24.2 us (11%)
  matrix products  15.6 us (7%)
  blocking collectives  9.05 us (4%)
    another operation x5, other arithmetic, chol_apply(): return jax.scipy.linalg.cho_solve((factor, True), right)  39.6 us
    scatter x2, local copies, waits for them, and re-layouts, finish_box(): return jnp.zeros_like(ordered).at[order].set(ordered)  26 us
    all_to_all x1, waiting for transfers between devices, per_device(): lax.all_to_all(jnp.stack([local_solve] * lax.axis_size('coarse')), 'coars...  25.8 us
    another operation x4, other arithmetic, factor_box(): schur_factor = jnp.linalg.cholesky(schur)  23.8 us
    another operation x3, other arithmetic, factor_box(): red_factor = jnp.linalg.cholesky(red_block)  23.6 us
    ppermute x4, starting transfers between devices, shifted_2(): return lax.ppermute(block, axis, route)  19.7 us
    all_gather x1, blocking collectives, per_device(): lax.all_gather(skeleton, 'coarse', axis=1, tiled=True)  9.05 us
    dot_general x1, matrix products, coarse_terms(): jnp.einsum('bckl,cln->bkn', blocks * weights[:, :, None, None], cand_rhs,...  7.26 us
  transfers between devices with their start and end apart: 5, of which 2 were waited for; matrix products, arithmetic and copies ran while one was open for 1% of the time, Pallas kernels for 0%

profile of v1, /device:TPU:249, one launch (start us, length us, event | category | flops | bytes accessed | tf_op | source)
XLA Modules:
  0.0 216.1 jit_solution(12918264524999419002)
XLA Ops:
  0.0 0.8 fusion.71
  0.8 0.7 fusion.74
  1.7 0.8 broadcast_add_fusion
  2.5 0.1 copy.103
  2.8 3.6 %gather_fusion = f32[512,3]{1,0:T(8,128)S(1)} fusion(f32[1,2,3,256]{2,3,1,0:T(8,128)S(1)} %copy.103, s32[512]{0:T(512)S(1)} %bitcast.205), kind=kCustom, calls=%fused_computation | custom fusion | bytes 18432 | tf_op jit(solution)/shard_map/vmap(vmap(jit(_take)))/gather | solution.py:38
  6.5 0.3 multiply_reduce_fusion.1
  6.8 0.2 copy.107
  7.1 4.7 %gather_fusion.1 = f32[512]{0:T(512)S(1)} fusion(f32[1,2,256]{2,1,0:T(2,128)S(1)} %copy-done.1, s32[512]{0:T(512)S(1)} %bitcast.206), kind=kCustom, calls=%fused_computation.1 | custom fusion | bytes 10240 | tf_op jit(solution)/shard_map/vmap(vmap(jit(_take)))/gather | solution.py:39
  12.0 0.3 fusion.25
  12.2 0.3 fusion.56
  12.6 0.4 fusion.24
  13.0 0.4 fusion.23
  13.5 23.5 %custom-call.27 = f32[1,2,128,128]{3,2,1,0:T(8,128)S(1)} custom-call(f32[1,2,128,128]{3,2,1,0:T(8,128)S(1)} %fusion.49), custom_call_target="Cholesky" | custom-call | tf_op jit(solution)/shard_map/vmap(vmap(jit(cholesky)))/cholesky | solution.py:54
  37.0 0.1 compare_reduce_fusion.1
  37.2 19.7 %custom-call.15 = f32[1,2,1,128,128]{3,4,2,1,0:T(8,128)S(1)} custom-call(f32[1,2,1,128,128]{4,3,2,1,0:T(8,128)S(1)} %fusion.59), custom_call_target="InvertDiagBlocksLowerTriangular" | custom-call | tf_op jit(solution)/shard_map/vmap(vmap(jit(_cho_solve)))/triangular_solve | solution.py:27
  56.9 0.4 fusion.47
  57.3 0.3 fusion.45
  57.6 0.4 fusion.26
  58.1 23.6 %custom-call.28 = f32[1,2,128,128]{3,2,1,0:T(8,128)S(1)} custom-call(f32[1,2,128,128]{3,2,1,0:T(8,128)S(1)} %fusion.41), custom_call_target="Cholesky" | custom-call | tf_op jit(solution)/shard_map/vmap(vmap(jit(cholesky)))/cholesky | solution.py:60
  81.8 0.1 compare_reduce_fusion
  82.0 19.7 %custom-call.29 = f32[1,2,1,128,128]{3,4,2,1,0:T(8,128)S(1)} custom-call(f32[1,2,1,128,128]{4,3,2,1,0:T(8,128)S(1)} %select_bitcast_fusion), custom_call_target="InvertDiagBlocksLowerTriangular" | custom-call | tf_op jit(solution)/shard_map/vmap(vmap(jit(_cho_solve)))/triangular_solve | solution.py:27
  101.7 3.9 %gather_fusion.2 = f32[512,512]{1,0:T(8,128)S(1)} fusion(f32[1,2,256,512]{3,2,1,0:T(8,128)S(1)} %copy-done, s32[512]{0:T(512)S(1)} %bitcast.207), kind=kCustom, calls=%fused_computation.2 | custom fusion | bytes 2103296 | tf_op jit(solution)/shard_map/vmap(vmap(jit(_take)))/gather | solution.py:40
  105.6 0.3 copy.119
  106.1 0.6 fusion.17
  106.6 0.2 copy-done.5
  106.9 0.6 fusion.19
  107.4 0.6 fusion.39
  108.1 0.6 fusion.37
  108.7 1.6 stack.5
  110.3 4.4 %all-to-all-start = ((f32[4,1,2,128,512]{4,3,2,1,0:T(8,128)}), f32[4,1,2,128,512]{4,3,2,1,0:T(8,128)}, u32[]{:S(2)}, u32[]{:S(2)}) async-start(f32[4,1,2,128,512]{4,3,2,1,0:T(8,128)} %stack.5), calls=%async_computation | async-start | bytes 4194304 | tf_op jit(solution)/shard_map/all_to_all | solution.py:112
  114.7 25.8 %all-to-all-done = f32[4,1,2,128,512]{4,3,2,1,0:T(8,128)} async-done(((f32[4,1,2,128,512]{4,3,2,1,0:T(8,128)}), f32[4,1,2,128,512]{4,3,2,1,0:T(8,128)}, u32[]{:S(2)}, u32[]{:S(2)}) %all-to-all-start) | async-done | bytes 2097184 | tf_op jit(solution)/shard_map/all_to_all | solution.py:112
  140.5 5.8 %collective-permute-start.2 = (f32[1,8,128,512]{3,2,1,0:T(8,128)}, f32[1,8,128,512]{3,2,1,0:T(8,128)S(1)}, u32[]{:S(2)}, u32[]{:S(2)}) collective-permute-start(f32[1,8,128,512]{3,2,1,0:T(8,128)} %bitcast.44), channel_id=1, source_target_pairs={{0,4},{4,8},{8,12},{12,16},{16,20},{20,24},{24,28},{28,32},{32,36}... | collective-permute-start | bytes 6291464 | tf_op jit(solution)/shard_map/ppermute | solution.py:14
  146.3 1.9 collective-permute-start.3
  148.3 9.0 %all_gather.3 = f32[1,8,3,128]{3,0,2,1:T(1,128)S(1)} all-gather(f32[1,2,3,128]{3,0,2,1:T(1,128)S(1)} %copy.126), channel_id=1, replica_groups=mesh['box'=128,'coarse'=4] {'coarse'}, dimensions={1}, use_global_device_ids=true | all-gather | bytes 15360 | tf_op jit(solution)/shard_map/all_gather | solution.py:115
  157.3 9.8 %collective-permute-start = (f32[1,8,3,128]{3,0,2,1:T(1,128)S(1)}, f32[1,8,3,128]{3,0,2,1:T(1,128)S(1)}, u32[]{:S(2)}, u32[]{:S(2)}) collective-permute-start(f32[1,8,3,128]{3,0,2,1:T(1,128)S(1)} %all_gather.3), channel_id=1, source_target_pairs={{0,4},{4,8},{8,12},{12,16},{16,20},{20,24},{24,28},{28,32},{32,36}... | collective-permute-start | bytes 36872 | tf_op jit(solution)/shard_map/ppermute | solution.py:14
  167.2 2.1 collective-permute-start.1
  169.6 0.6 fusion.43
  170.4 7.0 %collective-permute-done.1 = f32[1,8,3,128]{3,0,2,1:T(1,128)S(1)} collective-permute-done((f32[1,8,3,128]{3,0,2,1:T(1,128)S(1)}, f32[1,8,3,128]{3,0,2,1:T(1,128)S(1)}, u32[]{:S(2)}, u32[]{:S(2)}) %collective-permute-start.1) | collective-permute-done | bytes 12320 | tf_op jit(solution)/shard_map/ppermute | solution.py:14
  177.4 1.1 multiply_reduce_fusion
  178.6 7.3 %fusion.13 = f32[2,128,512]{2,1,0:T(8,128)S(1)} fusion(f32[1,8,128,512]{3,2,1,0:T(8,128)S(1)} %collective-permute-done.3, f32[1,8,128,512]{3,2,1,0:T(8,128)} %bitcast.44, f32[1,8,128,512]{3,2,1,0:T(8,128)S(1)} %collective-permute-done.2, f32[2,24,128,128]{3,2,1,0:T(8,128)S(1)} %multiply_reduce_fusion, f32[2,24]{1,0:T(2,128)S(1)} %maximum_bitcast_fusion.7), kind=kOutput, calls=%fused_computation.24 | convolution fusion | flops 4836687872 | bytes 9961664 | tf_op jit(solution)/shard_map/vmap(bckl,cln->bkn)/dot_general | solution.py:80
  185.8 0.6 fusion.35
  186.5 0.6 fusion.20
  187.1 0.6 convolution_bitcast_fusion.1
  187.7 0.6 fusion.21
  188.3 0.6 fusion.22
  189.0 0.1 broadcast.682
  189.1 26.0 %scatter_fusion = f32[2,256,512]{2,1,0:T(8,128)S(1)} fusion(f32[2,256,512]{2,1,0:T(8,128)S(1)} %broadcast.682, s32[512]{0:T(512)S(1)} %bitcast.208, f32[512,512]{1,0:T(8,128)S(1)} %bitcast.209), kind=kCustom, calls=%fused_computation.3 | custom fusion | bytes 3149824 | tf_op jit(solution)/shard_map/vmap(vmap())/scatter | solution.py:95
  215.1 1.0 copy-done.2
  (63 shorter events, 1.8 us)
Async XLA Ops:
  0.0 101.7 %copy-start = (f32[1,2,256,512]{3,2,1,0:T(8,128)S(1)}, f32[1,2,256,512]{3,2,1,0:T(8,128)}, u32[]{:S(2)}) copy-start(f32[1,2,256,512]{3,2,1,0:T(8,128)} %param.14) | copy-start | bytes 3145732
  0.0 11.8 %copy-start.6 = (s32[1,2,256]{2,1,0:T(2,128)S(1)}, s32[1,2,256]{2,1,0:T(2,128)}, u32[]{:S(2)}) copy-start(s32[1,2,256]{2,1,0:T(2,128)} %param.11) | copy-start | bytes 6148
  0.0 7.1 %copy-start.1 = (f32[1,2,256]{2,1,0:T(2,128)S(1)}, f32[1,2,256]{2,1,0:T(2,128)}, u32[]{:S(2)}) copy-start(f32[1,2,256]{2,1,0:T(2,128)} %param.10) | copy-start | bytes 6148
  2.7 9.3 %copy-start.3 = (f32[1,2,128,128]{3,2,1,0:T(8,128)S(1)}, f32[1,2,128,128]{3,2,1,0:T(8,128)}, u32[]{:S(2)}) copy-start(f32[1,2,128,128]{3,2,1,0:T(8,128)} %param.12) | copy-start | bytes 393220
  57.6 24.4 %copy-start.4 = (f32[2,128,128]{2,1,0:T(8,128)}, f32[2,128,128]{2,1,0:T(8,128)S(1)}, u32[]{:S(2)}) copy-start(f32[2,128,128]{2,1,0:T(8,128)S(1)} %fusion.45) | copy-start | bytes 393220
  106.0 0.9 copy-start.5
  108.7 60.7 %copy-start.7 = (s32[1,2,6]{2,1,0:T(2,128)S(1)}, s32[1,2,6]{2,1,0:T(2,128)}, u32[]{:S(2)}) copy-start(s32[1,2,6]{2,1,0:T(2,128)} %param.13) | copy-start | bytes 148
  110.3 30.3 %all-to-all-start = ((f32[4,1,2,128,512]{4,3,2,1,0:T(8,128)}), f32[4,1,2,128,512]{4,3,2,1,0:T(8,128)}, u32[]{:S(2)}, u32[]{:S(2)}) async-start(f32[4,1,2,128,512]{4,3,2,1,0:T(8,128)} %stack.5), calls=%async_computation | async-start | bytes 4194304 | tf_op jit(solution)/shard_map/all_to_all | solution.py:112
  140.5 38.0 %collective-permute-start.2 = (f32[1,8,128,512]{3,2,1,0:T(8,128)}, f32[1,8,128,512]{3,2,1,0:T(8,128)S(1)}, u32[]{:S(2)}, u32[]{:S(2)}) collective-permute-start(f32[1,8,128,512]{3,2,1,0:T(8,128)} %bitcast.44), channel_id=1, source_target_pairs={{0,4},{4,8},{8,12},{12,16},{16,20},{20,24},{24,28},{28,32},{32,36}... | collective-permute-start | bytes 6291464 | tf_op jit(solution)/shard_map/ppermute | solution.py:14
  146.3 32.2 %collective-permute-start.3 = (f32[1,8,128,512]{3,2,1,0:T(8,128)}, f32[1,8,128,512]{3,2,1,0:T(8,128)S(1)}, u32[]{:S(2)}, u32[]{:S(2)}) collective-permute-start(f32[1,8,128,512]{3,2,1,0:T(8,128)} %bitcast.44), channel_id=1, source_target_pairs={{4,0},{8,4},{12,8},{16,12},{20,16},{24,20},{28,24},{32,28},{36,32}... | collective-permute-start | bytes 6291464 | tf_op jit(solution)/shard_map/ppermute | solution.py:14
  157.3 13.0 %collective-permute-start = (f32[1,8,3,128]{3,0,2,1:T(1,128)S(1)}, f32[1,8,3,128]{3,0,2,1:T(1,128)S(1)}, u32[]{:S(2)}, u32[]{:S(2)}) collective-permute-start(f32[1,8,3,128]{3,0,2,1:T(1,128)S(1)} %all_gather.3), channel_id=1, source_target_pairs={{0,4},{4,8},{8,12},{12,16},{16,20},{20,24},{24,28},{28,32},{32,36}... | collective-permute-start | bytes 36872 | tf_op jit(solution)/shard_map/ppermute | solution.py:14
  167.2 10.2 %collective-permute-start.1 = (f32[1,8,3,128]{3,0,2,1:T(1,128)S(1)}, f32[1,8,3,128]{3,0,2,1:T(1,128)S(1)}, u32[]{:S(2)}, u32[]{:S(2)}) collective-permute-start(f32[1,8,3,128]{3,0,2,1:T(1,128)S(1)} %all_gather.3), channel_id=1, source_target_pairs={{4,0},{8,4},{12,8},{16,12},{20,16},{24,20},{28,24},{32,28},{36,32}... | collective-permute-start | bytes 36872 | tf_op jit(solution)/shard_map/ppermute | solution.py:14
  215.1 1.0 copy-start.2
